TPU v7x, 256 devices: a whole 4x4x8 slice. The times are simulated.
256 devices in a mesh: section: 2 (over z_hi), dp: 16 (over z_lo, y), tensor: 8 (over x, core).
Axes of the slice: x: 4, y: 4, z: 8 (z_hi: 2, z_lo: 4; z = z_hi * 4 + z_lo), core: 2. Of those that a mesh axis runs over, the one named last changes fastest.
Arguments:
- section_input: bfloat16 [2, 1024, 8192], P('section', 'tensor', 'dp'), may hold values from -40 to 40
- norm_gain_attn: bfloat16 [2, 8192], P('section', 'dp'), may hold values from 0.099609375 to 1.8984375
- w_query: bfloat16 [2, 8192, 4096], P('section', 'dp', 'tensor'), may hold values from -0.0625 to 0.0625
- key_value_weight: bfloat16 [2, 2, 8192, 512], P('section', None, 'dp'), may hold values from -0.0625 to 0.0625
- w_output: bfloat16 [2, 4096, 8192], P('section', 'tensor', 'dp'), may hold values from -0.09375 to 0.09375
- norm_gain_ffn: bfloat16 [2, 8192], P('section', 'dp'), may hold values from 0.099609375 to 1.8984375
- w_gate_up: bfloat16 [2, 2, 8192, 14336], P('section', None, 'dp', 'tensor'), may hold values from -0.0625 to 0.0625
- w_down: bfloat16 [2, 14336, 8192], P('section', 'tensor', 'dp'), may hold values from -0.046875 to 0.046875
Outputs:
- section_output: bfloat16 [2, 1024, 8192], P('section', 'tensor', 'dp')
All inputs are finite; a program needn't handle non-finite values.
Results may differ from a plain program's by a relative error of at most 0.019.
Values may be sent and summed in bfloat16 or wider, within the bound.
A program may use at most 64 MiB of HBM per device.

v0:
```python
import math
import jax
import jax.numpy as jnp
from jax import lax
from jax.sharding import PartitionSpec as P

HEAD_SIZE = 128
QUERY_HEADS = 32
KEY_VALUE_HEADS = 4
EPS = 1e-05
THETA = 500000.0


def from_behind(x, axis, by):
    count = lax.axis_size(axis)
    return lax.ppermute(x, axis, [(i, (i + by) % count) for i in range(count)])


def apply_rotary(value_states, token_positions):
    width = value_states.shape[-1]
    half = width // 2
    freqs = jnp.exp(-(2.0 * jnp.arange(half, dtype=jnp.float32) / width) * math.log(THETA))
    angles = token_positions.astype(jnp.float32)[:, None] * freqs[None, :]
    cosine = jnp.cos(angles)[:, None, :]
    sine = jnp.sin(angles)[:, None, :]
    first = value_states[..., :half]
    second = value_states[..., half:]
    return jnp.concatenate(
        [first * cosine - second * sine, second * cosine + first * sine], axis=-1
    )


def local(
    section_input,
    norm_gain_attn,
    w_query,
    key_value_weight,
    w_output,
    norm_gain_ffn,
    w_gate_up,
    w_down,
):
    tile = section_input[0]
    rows_dev = tile.shape[0]
    cols_dev = tile.shape[1]
    tensor_count = lax.axis_size("tensor")
    data_count = lax.axis_size("dp")
    seq_total = rows_dev * tensor_count
    query_rows = seq_total // data_count
    width_total = cols_dev * data_count
    head_dim = HEAD_SIZE
    heads_dev = w_query.shape[2] // head_dim
    group_heads = QUERY_HEADS // KEY_VALUE_HEADS
    kv_dev = max(1, heads_dev // group_heads)
    per_kv = heads_dev // kv_dev
    tensor_pos = lax.axis_index("tensor")
    data_pos = lax.axis_index("dp")
    kv_first = tensor_pos * heads_dev // group_heads
    key_cols = lax.dynamic_slice_in_dim(
        key_value_weight[0], kv_first * head_dim, kv_dev * head_dim, 2
    )
    w_columns = jnp.concatenate([w_query[0], key_cols[0], key_cols[1]], axis=1)
    gain_attn = norm_gain_attn[0].astype(jnp.float32)[None, :]
    gain_ffn = norm_gain_ffn[0].astype(jnp.float32)[None, :]
    query_cols = heads_dev * head_dim
    kv_cols = kv_dev * head_dim
    query_pos = data_pos * query_rows + jnp.arange(query_rows, dtype=jnp.int32)
    all_pos = jnp.arange(seq_total, dtype=jnp.int32)
    arrived = from_behind(tile, "section", 1)
    wide = arrived.astype(jnp.float32)
    squares = lax.psum(jnp.sum(wide * wide, axis=1), "dp")
    normed_input = (wide * lax.rsqrt(squares / width_total + EPS)[:, None] * gain_attn).astype(
        jnp.bfloat16
    )
    partial_qkv = jnp.dot(
        lax.all_gather(normed_input, "tensor", axis=0, tiled=True),
        w_columns,
        preferred_element_type=jnp.float32,
    )
    query_sum = lax.psum_scatter(
        partial_qkv[:, :query_cols].astype(jnp.bfloat16), "dp", scatter_dimension=0, tiled=True
    ).astype(jnp.float32)
    key_sum = lax.psum(partial_qkv[:, query_cols:].astype(jnp.bfloat16), "dp").astype(jnp.float32)
    keys = apply_rotary(key_sum[:, :kv_cols].reshape(seq_total, kv_dev, head_dim), all_pos).astype(
        jnp.bfloat16
    )
    value_states = key_sum[:, kv_cols:].reshape(seq_total, kv_dev, head_dim).astype(jnp.bfloat16)
    query_states = apply_rotary(
        query_sum.reshape(query_rows, heads_dev, head_dim), query_pos
    ).astype(jnp.bfloat16)
    grouped = query_states.reshape(query_rows, kv_dev, per_kv, head_dim)
    scores = jnp.einsum(
        "qkgd,skd->kgqs", grouped, keys, preferred_element_type=jnp.float32
    ) * head_dim ** (-0.5)
    visible = all_pos[None, :] <= query_pos[:, None]
    weights_exp = jnp.where(visible, jnp.exp(scores), 0.0)
    probs = (weights_exp / jnp.sum(weights_exp, axis=-1, keepdims=True)).astype(jnp.bfloat16)
    mixed = (
        jnp.einsum("kgqs,skd->qkgd", probs, value_states, preferred_element_type=jnp.float32)
        .astype(jnp.bfloat16)
        .reshape(query_rows, query_cols)
    )
    attn_partial = jnp.dot(
        lax.all_gather(mixed, "dp", axis=0, tiled=True),
        w_output[0],
        preferred_element_type=jnp.float32,
    )
    attn = lax.psum_scatter(
        attn_partial.astype(jnp.bfloat16), "tensor", scatter_dimension=0, tiled=True
    ).astype(jnp.float32)
    resid = (arrived.astype(jnp.float32) + attn).astype(jnp.bfloat16)
    resid_wide = resid.astype(jnp.float32)
    squares_ffn = lax.psum(jnp.sum(resid_wide * resid_wide, axis=1), "dp")
    normed_ffn = (
        resid_wide * lax.rsqrt(squares_ffn / width_total + EPS)[:, None] * gain_ffn
    ).astype(jnp.bfloat16)
    rows_ffn = lax.all_gather(normed_ffn, "tensor", axis=0, tiled=True)
    ff_dev = w_gate_up.shape[3]
    summed = lax.psum_scatter(
        jnp.einsum("rd,gdf->rgf", rows_ffn, w_gate_up[0], preferred_element_type=jnp.float32)
        .reshape(query_rows * lax.axis_size("dp"), 2 * ff_dev)
        .astype(jnp.bfloat16),
        "dp",
        scatter_dimension=0,
        tiled=True,
    ).astype(jnp.float32)
    hidden = (jax.nn.silu(summed[:, :ff_dev]) * summed[:, ff_dev:]).astype(jnp.bfloat16)
    ffn_partial = jnp.dot(
        lax.all_gather(hidden, "dp", axis=0, tiled=True),
        w_down[0],
        preferred_element_type=jnp.float32,
    )
    ffn = lax.psum_scatter(
        ffn_partial.astype(jnp.bfloat16), "tensor", scatter_dimension=0, tiled=True
    ).astype(jnp.float32)
    result = (resid_wide + ffn).astype(jnp.bfloat16)
    return result[None]


def solution(mesh):
    placed = (
        P("section", "tensor", "dp"),
        P("section", "dp"),
        P("section", "dp", "tensor"),
        P("section", None, "dp", None),
        P("section", "tensor", "dp"),
        P("section", "dp"),
        P("section", None, "dp", "tensor"),
        P("section", "tensor", "dp"),
    )
    return jax.shard_map(
        local, mesh=mesh, in_specs=placed, out_specs=P("section", "tensor", "dp"), check_vma=False
    )
```

profile of v0, /device:TPU:8, one launch (start us, length us, event | category | flops | bytes accessed | tf_op | source)
XLA Modules:
  0.0 766.1 jit_solution(4502816704359785971)
XLA Ops:
  6.5 7.2 collective-permute-start
  14.4 3.1 collective-permute-done
  17.6 38.6 %psum.21 = f32[128]{0:T(128)S(1)} all-reduce(f32[128]{0:T(128)S(1)} %fusion.25), channel_id=1, replica_groups=mesh['section'=2,'dp'=16,'tensor'=8] {'dp'}, use_global_device_ids=true, to_apply=%region_1.2 | all-reduce | flops 128 | bytes 1024 | tf_op jit(solution)/shard_map/psum | solution.py:71
  57.1 1.7 dynamic-slice_bitcast_fusion.1
  58.8 27.4 %all-gather.5.cloned.1.call-done = bf16[1024,512]{1,0:T(8,128)(2,1)} async-done(((bf16[128,512]{1,0:T(8,128)(2,1)}), bf16[1024,512]{1,0:T(8,128)(2,1)}) %all-gather.5.cloned.1.call-update) | async-done | bytes 1048592 | tf_op jit(solution)/shard_map/all_gather | solution.py:76
  86.2 2.4 convolution_convert_fusion.1
  91.1 160.4 %all-reduce.2.cloned.1.call-done = bf16[1024,256]{1,0:T(8,128)(2,1)} async-done(((bf16[1024,256]{1,0:T(8,128)(2,1)}), bf16[1024,256]{1,0:T(8,128)(2,1)}) %all-reduce.2.cloned.1.call-update) | async-done | bytes 524304 | tf_op jit(solution)/shard_map/psum | solution.py:83
  251.5 1.1 fusion.33
  252.6 2.4 fusion.37
  255.0 79.3 %reduce-scatter.5.cloned.1.call-done = bf16[64,512]{1,0:T(8,128)(2,1)} async-done(((bf16[1024,512]{1,0:T(8,128)(2,1)}), bf16[64,512]{1,0:T(8,128)(2,1)}) %reduce-scatter.5.cloned.1.call-update) | async-done | bytes 65552 | tf_op jit(solution)/shard_map/reduce_scatter | solution.py:80
  337.1 81.5 %all-gather.7.cloned.1.call-done = bf16[1024,512]{1,0:T(8,128)(2,1)} async-done(((bf16[64,512]{1,0:T(8,128)(2,1)}), bf16[1024,512]{1,0:T(8,128)(2,1)}) %all-gather.7.cloned.1.call-update) | async-done | bytes 1048592 | tf_op jit(solution)/shard_map/all_gather | solution.py:104
  418.6 3.0 convolution_convert_fusion.2
  421.8 33.3 %reduce-scatter.7.cloned.1.call-done = bf16[128,512]{1,0:T(8,128)(2,1)} async-done(((bf16[1024,512]{1,0:T(8,128)(2,1)}), bf16[128,512]{1,0:T(8,128)(2,1)}) %reduce-scatter.7.cloned.1.call-update) | async-done | bytes 131088 | tf_op jit(solution)/shard_map/reduce_scatter | solution.py:108
  456.1 39.0 %psum.23 = f32[128]{0:T(128)S(1)} all-reduce(f32[128]{0:T(128)S(1)} %fusion.29), channel_id=1, replica_groups=mesh['section'=2,'dp'=16,'tensor'=8] {'dp'}, use_global_device_ids=true, to_apply=%region_7.8 | all-reduce | flops 128 | bytes 1024 | tf_op jit(solution)/shard_map/psum | solution.py:113
  495.1 1.7 fusion.31
  496.8 6.0 copy.14
  502.8 18.1 %all-gather.9.cloned.1.call-done = bf16[1024,512]{1,0:T(8,128)(2,1)} async-done(((bf16[128,512]{1,0:T(8,128)(2,1)}), bf16[1024,512]{1,0:T(8,128)(2,1)}) %all-gather.9.cloned.1.call-update) | async-done | bytes 1048592 | tf_op jit(solution)/shard_map/all_gather | solution.py:117
  520.9 9.3 %convolution_convert_fusion = bf16[1024,3584]{1,0:T(8,128)(2,1)} fusion(bf16[1024,512]{1,0:T(8,128)(2,1)} %all-gather.9.cloned.1.call-done, bf16[3584,512]{1,0:T(8,128)(2,1)} %bitcast.64), kind=kOutput, calls=%fused_computation | convolution fusion | flops 3761766400 | bytes 12058624 | tf_op jit(solution)/shard_map/rd,gdf->rgf/dot_general | solution.py:120
  530.3 101.4 %reduce-scatter.9.cloned.1.call-done = bf16[64,3584]{1,0:T(8,128)(2,1)} async-done(((bf16[1024,3584]{1,0:T(8,128)(2,1)}), bf16[64,3584]{1,0:T(8,128)(2,1)}) %reduce-scatter.9.cloned.1.call-update) | async-done | bytes 458768 | tf_op jit(solution)/shard_map/reduce_scatter | solution.py:119
  631.7 1.1 convert_element_type.103
  633.7 85.8 %all-gather.11.cloned.1.call-done = bf16[1024,1792]{1,0:T(8,128)(2,1)} async-done(((bf16[64,1792]{1,0:T(8,128)(2,1)}), bf16[1024,1792]{1,0:T(8,128)(2,1)}) %all-gather.11.cloned.1.call-update) | async-done | bytes 3670032 | tf_op jit(solution)/shard_map/all_gather | solution.py:129
  719.4 5.1 fusion.2
  724.5 33.5 %reduce-scatter.11.cloned.1.call-done = bf16[128,512]{1,0:T(8,128)(2,1)} async-done(((bf16[1024,512]{1,0:T(8,128)(2,1)}), bf16[128,512]{1,0:T(8,128)(2,1)}) %reduce-scatter.11.cloned.1.call-update) | async-done | bytes 131088 | tf_op jit(solution)/shard_map/reduce_scatter | solution.py:133
  758.0 1.6 fusion.38
  (49 shorter events, 8.8 us)
Async XLA Ops:
  6.5 712.9 %copy-start = (bf16[1,1792,512]{2,1,0:T(8,128)(2,1)S(1)}, bf16[1,1792,512]{2,1,0:T(8,128)(2,1)}, u32[]{:S(2)}) copy-start(bf16[1,1792,512]{2,1,0:T(8,128)(2,1)} %param.15) | copy-start | bytes 5505028
  6.5 79.7 %all-gather.5.cloned.1.call-start = ((), (), s32[]{:S(2)}) async-start(), calls=%async_computation.4 | async-start | bytes 1179648 | tf_op jit(solution)/shard_map/all_gather | solution.py:76
  6.5 11.0 %collective-permute-start = (bf16[128,512]{1,0:T(8,128)(2,1)}, bf16[128,512]{1,0:T(8,128)(2,1)S(1)}, u32[]{:S(2)}, u32[]{:S(2)}) collective-permute-start(bf16[128,512]{1,0:T(8,128)(2,1)} %bitcast.70), channel_id=1, source_target_pairs={{0,128},{128,0},{1,129},{129,1},{2,130},{130,2},{3,131},{131,3},{4... | collective-permute-start | bytes 393224 | tf_op jit(solution)/shard_map/ppermute | solution.py:16
  57.0 194.5 %all-reduce.2.cloned.1.call-start = ((), (), s32[]{:S(2)}) async-start(), calls=%async_computation.5 | async-start | bytes 1048576 | tf_op jit(solution)/shard_map/psum | solution.py:83
  89.5 244.8 %reduce-scatter.5.cloned.1.call-start = ((), (), s32[]{:S(2)}) async-start(), calls=%async_computation.6 | async-start | bytes 1114112 | tf_op jit(solution)/shard_map/reduce_scatter | solution.py:80
  90.7 328.0 %all-gather.7.cloned.1.call-start = ((), (), s32[]{:S(2)}) async-start(), calls=%async_computation.7 | async-start | bytes 1114112 | tf_op jit(solution)/shard_map/all_gather | solution.py:104
  251.5 84.5 %copy-start.2 = (bf16[1024,256]{1,0:T(8,128)(2,1)S(1)}, bf16[1024,256]{1,0:T(8,128)(2,1)}, u32[]{:S(2)}) copy-start(bf16[1024,256]{1,0:T(8,128)(2,1)} %all-reduce.2.cloned.1.call-done) | copy-start | bytes 1572868
  336.3 85.4 %copy-start.3 = (bf16[1,512]{1,0:T(2,128)(2,1)S(1)}, bf16[1,512]{1,0:T(2,128)(2,1)}, u32[]{:S(2)}) copy-start(bf16[1,512]{1,0:T(2,128)(2,1)} %param.13) | copy-start | bytes 3076
  337.1 118.0 %reduce-scatter.7.cloned.1.call-start = ((), (), s32[]{:S(2)}) async-start(), calls=%async_computation.8 | async-start | bytes 1179648 | tf_op jit(solution)/shard_map/reduce_scatter | solution.py:108
  421.7 99.2 %all-gather.9.cloned.1.call-start = ((), (), s32[]{:S(2)}) async-start(), calls=%async_computation.9 | async-start | bytes 1179648 | tf_op jit(solution)/shard_map/all_gather | solution.py:117
  496.7 134.9 %reduce-scatter.9.cloned.1.call-start = ((), (), s32[]{:S(2)}) async-start(), calls=%async_computation.10 | async-start | bytes 7798784 | tf_op jit(solution)/shard_map/reduce_scatter | solution.py:119
  530.3 189.1 %all-gather.11.cloned.1.call-start = ((), (), s32[]{:S(2)}) async-start(), calls=%async_computation.11 | async-start | bytes 3899392 | tf_op jit(solution)/shard_map/all_gather | solution.py:129
  633.6 124.4 %copy-start.1 = (bf16[128,512]{1,0:T(8,128)(2,1)S(1)}, bf16[128,512]{1,0:T(8,128)(2,1)}, u32[]{:S(2)}) copy-start(bf16[128,512]{1,0:T(8,128)(2,1)} %reduce-scatter.7.cloned.1.call-done) | copy-start | bytes 393220
  633.6 124.4 %reduce-scatter.11.cloned.1.call-start = ((), (), s32[]{:S(2)}) async-start(), calls=%async_computation.12 | async-start | bytes 1179648 | tf_op jit(solution)/shard_map/reduce_scatter | solution.py:133
Sparse Core Ops, SparseCore 0:
  57.2 29.0 all-gather.4
  89.7 161.8 all-reduce.1
  254.0 80.2 reduce-scatter.4
  337.2 81.3 all-gather.6
  421.8 33.1 reduce-scatter.6
  496.9 24.0 all-gather.8
  530.4 101.2 reduce-scatter.8
  633.7 85.6 all-gather.10
  724.7 33.2 reduce-scatter.10
where the time goes:
time: 767 us; the launch traced here: 766 us
  waiting for transfers between devices  624 us (81%)
  blocking collectives  77.6 us (10%)
  matrix products  20.8 us (3%)
  between operations  13.4 us (2%)
  other arithmetic  11.6 us (2%)
  local copies, waits for them, and re-layouts  11.3 us (1%)
    psum x1, waiting for transfers between devices, local(): lax.psum(partial_qkv[:, query_cols:].astype(jnp.bfloat16), 'dp')  160 us
    reduce_scatter x1, waiting for transfers between devices, local(): lax.psum_scatter(jnp.einsum('rd,gdf->rgf', rows_ffn, w_gate_up[0], prefer...  101 us
    all_gather x1, waiting for transfers between devices, local(): lax.all_gather(hidden, 'dp', axis=0, tiled=True)  85.8 us
    all_gather x1, waiting for transfers between devices, local(): lax.all_gather(mixed, 'dp', axis=0, tiled=True)  81.5 us
    reduce_scatter x1, waiting for transfers between devices, local(): lax.psum_scatter(partial_qkv[:, :query_cols].astype(jnp.bfloat16), 'dp',...  79.3 us
    psum x1, blocking collectives, local(): squares_ffn = lax.psum(jnp.sum(resid_wide * resid_wide, axis=1), 'dp')  39 us
    psum x1, blocking collectives, local(): squares = lax.psum(jnp.sum(wide * wide, axis=1), 'dp')  38.6 us
    reduce_scatter x1, waiting for transfers between devices, local(): lax.psum_scatter(ffn_partial.astype(jnp.bfloat16), 'tensor', scatter_dime...  33.5 us
  transfers between devices with their start and end apart: 10, of which 10 were waited for; matrix products, arithmetic and copies ran while one was open for 2% of the time, Pallas kernels for 0%

commit v1 on v0

--- a/solution.py
+++ b/solution.py
@@ -80,7 +80,11 @@
     query_sum = lax.psum_scatter(
         partial_qkv[:, :query_cols].astype(jnp.bfloat16), "dp", scatter_dimension=0, tiled=True
     ).astype(jnp.float32)
-    key_sum = lax.psum(partial_qkv[:, query_cols:].astype(jnp.bfloat16), "dp").astype(jnp.float32)
+    key_sum = (
+        lax.all_gather(partial_qkv[:, query_cols:].astype(jnp.bfloat16), axis_name="dp")
+        .sum(axis=0)
+        .astype(jnp.float32)
+    )
     keys = apply_rotary(key_sum[:, :kv_cols].reshape(seq_total, kv_dev, head_dim), all_pos).astype(
         jnp.bfloat16
     )

time: 767 us -> 711 us (0.927)
  waiting for transfers between devices: 624 us -> 564 us
    psum x1 -> x0, waiting for transfers between devices: 160 us -> none  [local(): lax.psum(partial_qkv[:, query_cols:].astype(jnp.bfloat16), 'dp')]
    all_gather x0 -> x1, waiting for transfers between devices: none -> 102 us  [local(): lax.all_gather(partial_qkv[:, query_cols:].astype(jnp.bfloat16), axis_nam...]
  transfers between devices with their start and end apart: 10 -> 10, of which waited for: 10 -> 10; matrix products, arithmetic and copies ran while one was open for 2% -> 1% of each run, Pallas kernels for 0% -> 0%
where the time goes in v1:
time: 711 us; the launch traced here: 710 us
  waiting for transfers between devices  564 us (79%)
  blocking collectives  77.6 us (11%)
  matrix products  20.7 us (3%)
  other arithmetic  15.4 us (2%)
  between operations  13.4 us (2%)
  local copies, waits for them, and re-layouts  11.4 us (2%)
  starting transfers between devices  7.53 us (1%)
    all_gather x1, waiting for transfers between devices, local(): lax.all_gather(partial_qkv[:, query_cols:].astype(jnp.bfloat16), axis_nam...  102 us
    reduce_scatter x1, waiting for transfers between devices, local(): lax.psum_scatter(jnp.einsum('rd,gdf->rgf', rows_ffn, w_gate_up[0], prefer...  101 us
    all_gather x1, waiting for transfers between devices, local(): lax.all_gather(hidden, 'dp', axis=0, tiled=True)  85.9 us
    reduce_scatter x1, waiting for transfers between devices, local(): lax.psum_scatter(partial_qkv[:, :query_cols].astype(jnp.bfloat16), 'dp',...  80.5 us
    all_gather x1, waiting for transfers between devices, local(): lax.all_gather(mixed, 'dp', axis=0, tiled=True)  79.7 us
    psum x1, blocking collectives, local(): squares_ffn = lax.psum(jnp.sum(resid_wide * resid_wide, axis=1), 'dp')  39 us
    psum x1, blocking collectives, local(): squares = lax.psum(jnp.sum(wide * wide, axis=1), 'dp')  38.6 us
    reduce_scatter x1, waiting for transfers between devices, local(): lax.psum_scatter(ffn_partial.astype(jnp.bfloat16), 'tensor', scatter_dime...  33.5 us
  transfers between devices with their start and end apart: 10, of which 10 were waited for; matrix products, arithmetic and copies ran while one was open for 1% of the time, Pallas kernels for 0%

profile of v1, /device:TPU:8, one launch (start us, length us, event | category | flops | bytes accessed | tf_op | source)
XLA Modules:
  0.0 710.2 jit_solution(13667671796648693740)
XLA Ops:
  6.5 7.2 %collective-permute-start = (bf16[128,512]{1,0:T(8,128)(2,1)}, bf16[128,512]{1,0:T(8,128)(2,1)S(1)}, u32[]{:S(2)}, u32[]{:S(2)}) collective-permute-start(bf16[128,512]{1,0:T(8,128)(2,1)} %bitcast.72), channel_id=1, source_target_pairs={{0,128},{128,0},{1,129},{129,1},{2,130},{130,2},{3,131},{131,3},{4... | collective-permute-start | bytes 393224 | tf_op jit(solution)/shard_map/ppermute | solution.py:16
  14.4 3.1 collective-permute-done
  17.6 38.6 %psum.14 = f32[128]{0:T(128)S(1)} all-reduce(f32[128]{0:T(128)S(1)} %fusion.25), channel_id=1, replica_groups=mesh['section'=2,'dp'=16,'tensor'=8] {'dp'}, use_global_device_ids=true, to_apply=%region_1.2 | all-reduce | flops 128 | bytes 1024 | tf_op jit(solution)/shard_map/psum | solution.py:71
  57.1 1.7 dynamic-slice_bitcast_fusion.1
  58.8 27.4 %all-gather.7.cloned.1.call-done = bf16[1024,512]{1,0:T(8,128)(2,1)} async-done(((bf16[128,512]{1,0:T(8,128)(2,1)}), bf16[1024,512]{1,0:T(8,128)(2,1)}) %all-gather.7.cloned.1.call-update) | async-done | bytes 1048592 | tf_op jit(solution)/shard_map/all_gather | solution.py:76
  86.2 2.4 convolution_convert_fusion.1
  88.7 1.1 slice.59
  91.2 80.5 %reduce-scatter.5.cloned.1.call-done = bf16[64,512]{1,0:T(8,128)(2,1)} async-done(((bf16[1024,512]{1,0:T(8,128)(2,1)}), bf16[64,512]{1,0:T(8,128)(2,1)}) %reduce-scatter.5.cloned.1.call-update) | async-done | bytes 65552 | tf_op jit(solution)/shard_map/reduce_scatter | solution.py:80
  172.7 101.7 %all-gather.15.cloned.1.call-done = bf16[16384,256]{1,0:T(8,128)(2,1)} async-done(((bf16[1024,256]{1,0:T(8,128)(2,1)}), bf16[16384,256]{1,0:T(8,128)(2,1)}) %all-gather.15.cloned.1.call-update) | async-done | bytes 8388624 | tf_op jit(solution)/shard_map/all_gather | solution.py:84
  274.4 4.8 reduce_sum.40
  279.3 2.4 fusion.37
  283.4 79.7 %all-gather.9.cloned.1.call-done = bf16[1024,512]{1,0:T(8,128)(2,1)} async-done(((bf16[64,512]{1,0:T(8,128)(2,1)}), bf16[1024,512]{1,0:T(8,128)(2,1)}) %all-gather.9.cloned.1.call-update) | async-done | bytes 1048592 | tf_op jit(solution)/shard_map/all_gather | solution.py:108
  363.1 2.9 convolution_convert_fusion.2
  366.1 33.3 %reduce-scatter.7.cloned.1.call-done = bf16[128,512]{1,0:T(8,128)(2,1)} async-done(((bf16[1024,512]{1,0:T(8,128)(2,1)}), bf16[128,512]{1,0:T(8,128)(2,1)}) %reduce-scatter.7.cloned.1.call-update) | async-done | bytes 131088 | tf_op jit(solution)/shard_map/reduce_scatter | solution.py:112
  400.4 39.0 %psum.15 = f32[128]{0:T(128)S(1)} all-reduce(f32[128]{0:T(128)S(1)} %fusion.29), channel_id=1, replica_groups=mesh['section'=2,'dp'=16,'tensor'=8] {'dp'}, use_global_device_ids=true, to_apply=%region_7.8 | all-reduce | flops 128 | bytes 1024 | tf_op jit(solution)/shard_map/psum | solution.py:117
  439.4 1.7 fusion.31
  441.1 6.0 copy.14
  447.1 18.2 %all-gather.11.cloned.1.call-done = bf16[1024,512]{1,0:T(8,128)(2,1)} async-done(((bf16[128,512]{1,0:T(8,128)(2,1)}), bf16[1024,512]{1,0:T(8,128)(2,1)}) %all-gather.11.cloned.1.call-update) | async-done | bytes 1048592 | tf_op jit(solution)/shard_map/all_gather | solution.py:121
  465.3 9.3 %convolution_convert_fusion = bf16[1024,3584]{1,0:T(8,128)(2,1)} fusion(bf16[1024,512]{1,0:T(8,128)(2,1)} %all-gather.11.cloned.1.call-done, bf16[3584,512]{1,0:T(8,128)(2,1)} %bitcast.66), kind=kOutput, calls=%fused_computation | convolution fusion | flops 3761766400 | bytes 12058624 | tf_op jit(solution)/shard_map/rd,gdf->rgf/dot_general | solution.py:124
  474.7 100.9 %reduce-scatter.9.cloned.1.call-done = bf16[64,3584]{1,0:T(8,128)(2,1)} async-done(((bf16[1024,3584]{1,0:T(8,128)(2,1)}), bf16[64,3584]{1,0:T(8,128)(2,1)}) %reduce-scatter.9.cloned.1.call-update) | async-done | bytes 458768 | tf_op jit(solution)/shard_map/reduce_scatter | solution.py:123
  577.5 85.9 %all-gather.13.cloned.1.call-done = bf16[1024,1792]{1,0:T(8,128)(2,1)} async-done(((bf16[64,1792]{1,0:T(8,128)(2,1)}), bf16[1024,1792]{1,0:T(8,128)(2,1)}) %all-gather.13.cloned.1.call-update) | async-done | bytes 3670032 | tf_op jit(solution)/shard_map/all_gather | solution.py:133
  663.5 5.1 fusion.2
  668.6 33.5 %reduce-scatter.11.cloned.1.call-done = bf16[128,512]{1,0:T(8,128)(2,1)} async-done(((bf16[1024,512]{1,0:T(8,128)(2,1)}), bf16[128,512]{1,0:T(8,128)(2,1)}) %reduce-scatter.11.cloned.1.call-update) | async-done | bytes 131088 | tf_op jit(solution)/shard_map/reduce_scatter | solution.py:137
  702.0 1.6 fusion.38
  (49 shorter events, 8.9 us)
Async XLA Ops:
  6.5 656.9 %copy-start = (bf16[1,1792,512]{2,1,0:T(8,128)(2,1)S(1)}, bf16[1,1792,512]{2,1,0:T(8,128)(2,1)}, u32[]{:S(2)}) copy-start(bf16[1,1792,512]{2,1,0:T(8,128)(2,1)} %param.15) | copy-start | bytes 5505028
  6.5 79.7 %all-gather.7.cloned.1.call-start = ((), (), s32[]{:S(2)}) async-start(), calls=%async_computation.4 | async-start | bytes 1179648 | tf_op jit(solution)/shard_map/all_gather | solution.py:76
  6.5 11.0 %collective-permute-start = (bf16[128,512]{1,0:T(8,128)(2,1)}, bf16[128,512]{1,0:T(8,128)(2,1)S(1)}, u32[]{:S(2)}, u32[]{:S(2)}) collective-permute-start(bf16[128,512]{1,0:T(8,128)(2,1)} %bitcast.72), channel_id=1, source_target_pairs={{0,128},{128,0},{1,129},{129,1},{2,130},{130,2},{3,131},{131,3},{4... | collective-permute-start | bytes 393224 | tf_op jit(solution)/shard_map/ppermute | solution.py:16
  57.0 114.6 %reduce-scatter.5.cloned.1.call-start = ((), (), s32[]{:S(2)}) async-start(), calls=%async_computation.5 | async-start | bytes 1114112 | tf_op jit(solution)/shard_map/reduce_scatter | solution.py:80
  89.8 184.6 %all-gather.15.cloned.1.call-start = ((), (), s32[]{:S(2)}) async-start(), calls=%async_computation.12 | async-start | bytes 8912896 | tf_op jit(solution)/shard_map/all_gather | solution.py:84
  90.7 272.4 %all-gather.9.cloned.1.call-start = ((), (), s32[]{:S(2)}) async-start(), calls=%async_computation.6 | async-start | bytes 1114112 | tf_op jit(solution)/shard_map/all_gather | solution.py:108
  281.7 81.4 %copy-start.3 = (bf16[1,512,512]{2,1,0:T(8,128)(2,1)S(1)}, bf16[1,512,512]{2,1,0:T(8,128)(2,1)}, u32[]{:S(2)}) copy-start(bf16[1,512,512]{2,1,0:T(8,128)(2,1)} %param.12) | copy-start | bytes 1572868
  282.6 83.5 %copy-start.2 = (bf16[1,512]{1,0:T(2,128)(2,1)S(1)}, bf16[1,512]{1,0:T(2,128)(2,1)}, u32[]{:S(2)}) copy-start(bf16[1,512]{1,0:T(2,128)(2,1)} %param.13) | copy-start | bytes 3076
  283.4 116.0 %reduce-scatter.7.cloned.1.call-start = ((), (), s32[]{:S(2)}) async-start(), calls=%async_computation.7 | async-start | bytes 1179648 | tf_op jit(solution)/shard_map/reduce_scatter | solution.py:112
  366.1 99.3 %all-gather.11.cloned.1.call-start = ((), (), s32[]{:S(2)}) async-start(), calls=%async_computation.8 | async-start | bytes 1179648 | tf_op jit(solution)/shard_map/all_gather | solution.py:121
  441.1 134.5 %reduce-scatter.9.cloned.1.call-start = ((), (), s32[]{:S(2)}) async-start(), calls=%async_computation.9 | async-start | bytes 7798784 | tf_op jit(solution)/shard_map/reduce_scatter | solution.py:123
  474.6 188.8 %all-gather.13.cloned.1.call-start = ((), (), s32[]{:S(2)}) async-start(), calls=%async_computation.10 | async-start | bytes 3899392 | tf_op jit(solution)/shard_map/all_gather | solution.py:133
  577.5 124.5 %copy-start.1 = (bf16[128,512]{1,0:T(8,128)(2,1)S(1)}, bf16[128,512]{1,0:T(8,128)(2,1)}, u32[]{:S(2)}) copy-start(bf16[128,512]{1,0:T(8,128)(2,1)} %reduce-scatter.7.cloned.1.call-done) | copy-start | bytes 393220
  577.5 124.5 %reduce-scatter.11.cloned.1.call-start = ((), (), s32[]{:S(2)}) async-start(), calls=%async_computation.11 | async-start | bytes 1179648 | tf_op jit(solution)/shard_map/reduce_scatter | solution.py:137
Sparse Core Ops, SparseCore 0:
  57.2 29.0 all-gather.6
  90.0 81.6 reduce-scatter.4
  173.4 100.9 all-gather.14
  283.5 79.5 all-gather.8
  366.2 33.1 reduce-scatter.6
  441.2 24.0 all-gather.10
  474.7 100.7 reduce-scatter.8
  577.6 85.8 all-gather.12
  668.7 33.2 reduce-scatter.10
